TPU v7x, 256 devices: a whole 4x4x8 slice. The times are simulated.
256 devices in a mesh: seq: 32 (over y, x, core), exp: 8 (over z).
Axes of the slice: x: 4, y: 4, z: 8, core: 2. Of those that a mesh axis runs over, the one named last changes fastest.
Arguments:
- mixer_input: bfloat16 [4096, 8192], P('seq', 'exp'), may hold values from -6 to 6
- gate_input: bfloat16 [4096, 8192], P('seq', 'exp'), may hold values from -6 to 6
- delta_raw: bfloat16 [4096, 8192], P('seq', 'exp'), may hold values from -7 to 16387
- input_coef: bfloat16 [4096, 16], P('seq'), may hold values from 0.19921875 to 1.796875
- output_coef: bfloat16 [4096, 16], P('seq'), may hold values from -3 to 3
- decay_rate: float32 [16, 8192], P(None, 'exp'), may hold values from 4.8828125e-06 to 0.05
- conv_weight: float32 [4, 8192], P(None, 'exp'), may hold values from -3 to 3
- conv_bias: float32 [8192], P('exp'), may hold values from -3 to 3
- skip_gain: float32 [8192], P('exp'), may hold values from 0.5 to 1.5
- out_weight: bfloat16 [8192, 4096], P('exp', 'seq'), may hold values from -0.0625 to 0.0625
- residual: bfloat16 [4096, 4096], P(('seq', 'exp')), may hold values from -6 to 6
- norm_gain: float32 [4096], replicated, may hold values from 0.1 to 1.9
- router_weight: bfloat16 [4096, 8], replicated, may hold values from -0.09375 to 0.09375
- expert_ids: int32 [4096, 2], P(('seq', 'exp')), may hold values from 0 to 7, all different within a row; in each aligned block of 16 rows (0 to 15, 16 to 31, ...) at most 5 rows name the same one
- gate_weight: bfloat16 [8, 4096, 12288], P('exp', None, 'seq'), may hold values from -0.09375 to 0.09375
- up_weight: bfloat16 [8, 4096, 12288], P('exp', None, 'seq'), may hold values from -0.09375 to 0.09375
- down_weight: bfloat16 [8, 12288, 4096], P('exp', 'seq'), may hold values from -0.0546875 to 0.0546875
Outputs:
- mixed: bfloat16 [4096, 8192], P('seq', 'exp')
- final: bfloat16 [4096, 4096], P(('seq', 'exp'))
Inputs may be any that keep to these rules, and one draw needn't show every extreme that they name: `expert_ids`: each row names two different experts. In each aligned block of 16 rows (the rows of one device) no expert is named by more than 5 rows, and in some block one expert is named by exactly 5 rows.
All inputs are finite; a program needn't handle non-finite values.
Results may differ from a plain program's by a relative error of at most 0.015.
Values may be sent and summed in bfloat16 or wider, within the bound.
No kernel may reach another device: no remote copies, remote signals or barrier semaphores. Data moves between devices by JAX's collectives and lax.ppermute only.
A program may use at most 128 MiB of HBM per device.

v0:
```python
import jax
import jax.numpy as jnp
from jax import lax
from jax.sharding import PartitionSpec as P

KCONV = 4


def from_behind(block, axis, distance):
    devices = range(lax.axis_size(axis))
    route = [(i - distance, i) for i in devices if i - distance in devices]
    return lax.ppermute(block, axis, route)


def carried_in(part, axis, combine, identity):
    place = lax.axis_index(axis)
    gathered = jax.tree.map(lambda a: lax.all_gather(a, axis), part)
    state = jax.tree.map(lambda a, e: jnp.zeros_like(a) + jnp.asarray(e, a.dtype), part, identity)

    def one(turn, state):
        return combine(
            state, jax.tree.map(lambda a: lax.dynamic_index_in_dim(a, turn, 0, False), gathered)
        )

    return lax.fori_loop(0, place, one, state)


def sweep(state, delta, convolved, input_rows, output_rows, decay_rate):

    def advance(carry, inputs):
        delta_row, value_row, input_row, output_row = inputs
        retain = jnp.exp(-delta_row[None, :] * decay_rate)
        carry = retain * carry + (1.0 - retain) * input_row[:, None] * value_row[None, :]
        return (carry, jnp.sum(output_row[:, None] * carry, axis=0))

    return lax.scan(advance, state, (delta, convolved, input_rows, output_rows), unroll=8)


def chain(earlier, later):
    return (earlier[0] * later[0], later[0] * earlier[1] + later[1])


def shards(
    mixer_input,
    gate_input,
    delta_raw,
    input_coef,
    output_coef,
    decay_rate,
    conv_weight,
    conv_bias,
    skip_gain,
    out_weight,
    residual,
    norm_gain,
    router_weight,
    expert_ids,
    gate_weight,
    up_weight,
    down_weight,
):
    length = mixer_input.shape[0]
    width = mixer_input.shape[1]
    tail = mixer_input[length - (KCONV - 1) :]
    before = from_behind(tail, "seq", 1)
    padded = jnp.concatenate([before, mixer_input], axis=0).astype(jnp.float32)
    summed = jnp.broadcast_to(conv_bias[None, :], (length, width))
    for offset in range(KCONV):
        summed = summed + conv_weight[offset][None, :] * padded[offset : offset + length]
    convolved = jax.nn.silu(summed)
    delta = jax.nn.softplus(delta_raw.astype(jnp.float32))
    input_rows = input_coef.astype(jnp.float32)
    output_rows = output_coef.astype(jnp.float32)
    zero_state = jnp.zeros(decay_rate.shape, jnp.float32)
    end_state, local_out = sweep(zero_state, delta, convolved, input_rows, output_rows, decay_rate)
    block_decay = jnp.exp(-jnp.sum(delta, axis=0)[None, :] * decay_rate)
    carried_decay, start_state = carried_in(
        (block_decay, end_state), "seq", chain, (jnp.ones_like(block_decay), zero_state)
    )
    last_state, scan_out = sweep(start_state, delta, convolved, input_rows, output_rows, decay_rate)
    mixed = (
        (scan_out + skip_gain[None, :] * convolved) * jax.nn.silu(gate_input.astype(jnp.float32))
    ).astype(jnp.bfloat16)
    rows = residual.shape[0]
    model_width = residual.shape[1]
    full_weight = lax.all_gather(out_weight, "seq", axis=1, tiled=True)
    projected = lax.psum_scatter(
        jnp.dot(mixed, full_weight, preferred_element_type=jnp.float32).astype(jnp.bfloat16),
        "exp",
        scatter_dimension=0,
        tiled=True,
    ).astype(jnp.float32)
    hidden_state = residual.astype(jnp.float32) + projected
    scale = lax.rsqrt(jnp.mean(hidden_state * hidden_state, axis=1, keepdims=True) + 1e-06)
    normed = (hidden_state * scale * norm_gain[None, :]).astype(jnp.bfloat16)
    experts = router_weight.shape[1]
    capacity = 2 * rows // experts + 1
    logits = jnp.dot(normed, router_weight, preferred_element_type=jnp.float32)
    expert_range = jnp.arange(experts, dtype=jnp.int32)
    matches = expert_ids[:, :, None] == expert_range[None, None, :]
    chosen = jnp.sum(jnp.where(matches, logits[:, None, :], 0.0), axis=2)
    first = jax.nn.sigmoid(chosen[:, 0] - chosen[:, 1])
    flat_ids = expert_ids.reshape(-1)
    position = jnp.arange(flat_ids.shape[0], dtype=jnp.int32)
    earlier = (flat_ids[:, None] == flat_ids[None, :]) & (position[None, :] < position[:, None])
    rank = jnp.sum(earlier.astype(jnp.int32), axis=1)
    target = flat_ids * capacity + rank
    placing = (jnp.arange(experts * capacity, dtype=jnp.int32)[:, None] == target[None, :]).astype(
        jnp.bfloat16
    )
    repeated = jnp.broadcast_to(normed[:, None, :], (rows, 2, model_width)).reshape(-1, model_width)
    outgoing = (
        jnp.dot(placing, repeated, preferred_element_type=jnp.float32)
        .astype(jnp.bfloat16)
        .reshape(experts, capacity, model_width)
    )
    arrived = lax.all_to_all(outgoing, "exp", split_axis=0, concat_axis=0, tiled=True)
    flat_rows = arrived.reshape(-1, arrived.shape[2])
    piece = lax.all_gather(flat_rows, "seq", axis=0, tiled=True)
    gating = jnp.dot(piece, gate_weight[0], preferred_element_type=jnp.float32)
    upward = jnp.dot(piece, up_weight[0], preferred_element_type=jnp.float32)
    activated = (jax.nn.silu(gating) * upward).astype(jnp.bfloat16)
    partial_out = jnp.dot(activated, down_weight[0], preferred_element_type=jnp.float32)
    summed_out = lax.psum_scatter(
        partial_out.astype(jnp.bfloat16), "seq", scatter_dimension=0, tiled=True
    )
    returned = lax.all_to_all(
        summed_out.reshape(arrived.shape), "exp", split_axis=0, concat_axis=0, tiled=True
    )
    flat_returned = returned.reshape(-1, model_width)
    picked = jnp.einsum(
        "sa,sd->ad", placing, flat_returned, preferred_element_type=jnp.float32
    ).reshape(rows, 2, model_width)
    moe_out = first[:, None] * picked[:, 0] + (1.0 - first)[:, None] * picked[:, 1]
    final = (hidden_state + moe_out).astype(jnp.bfloat16)
    return (mixed, final)


def solution(mesh):
    return jax.shard_map(
        shards,
        mesh=mesh,
        in_specs=(
            P("seq", "exp"),
            P("seq", "exp"),
            P("seq", "exp"),
            P("seq", None),
            P("seq", None),
            P(None, "exp"),
            P(None, "exp"),
            P("exp"),
            P("exp"),
            P("exp", "seq"),
            P(("seq", "exp"), None),
            P(),
            P(),
            P(("seq", "exp"), None),
            P("exp", None, "seq"),
            P("exp", None, "seq"),
            P("exp", "seq", None),
        ),
        out_specs=(P("seq", "exp"), P(("seq", "exp"), None)),
        check_vma=False,
    )
```

profile of v0, /device:TPU:2, one launch (start us, length us, event | category | flops | bytes accessed | tf_op | source)
XLA Modules:
  0.0 486.0 jit_solution(3095711971764541297)
XLA Ops:
  8.1 2.0 collective-permute-start
  10.2 2.1 fusion.59
  12.2 1.5 multiply_exponential_fusion
  17.3 1.8 fusion.81
  19.2 24.8 %while.37 = (s32[]{:T(128)}, f32[16,1024]{1,0:T(8,128)S(1)}, f32[16,8,1024]{2,1,0:T(8,128)}, f32[16,1024]{1,0:T(8,128)S(1)}, f32[16,8,16]{2,1,0:T(8,128)S(1)}, /...) while((s32[]{:T(128)}, f32[16,1024]{1,0:T(8,128)S(1)}, ...), condition=%wide.region_2.3_spmd.clone, body=%wide.region_1.2_spmd.clone.sunk | while | flops 811018 | bytes 396055 | solution.py:36
  22.3 1.4 constant_dynamic-slice_fusion.41
  30.0 1.5 constant_dynamic-slice_fusion.41
  31.8 1.3 constant_dynamic-slice_fusion.41
  34.8 1.3 constant_dynamic-slice_fusion.41
  45.6 20.6 %all-gather.11.cloned.1.call-done = f32[512,1024]{1,0:T(8,128)} async-done(((f32[16,1024]{1,0:T(8,128)}), f32[512,1024]{1,0:T(8,128)}) %all-gather.11.cloned.1.call-update) | async-done | bytes 2097168 | tf_op jit(solution)/shard_map/all_gather | solution.py:17
  66.2 51.3 %all-gather.13.cloned.1.call-done = f32[512,1024]{1,0:T(8,128)} async-done(((f32[16,1024]{1,0:T(8,128)}), f32[512,1024]{1,0:T(8,128)}) %all-gather.13.cloned.1.call-update) | async-done | bytes 2097168 | tf_op jit(solution)/shard_map/all_gather | solution.py:17
  117.5 1.8 while.35
  119.4 40.2 %while.36 = (s32[]{:T(128)}, f32[16,1024]{1,0:T(8,128)S(1)}, f32[16,8,1024]{2,1,0:T(8,128)}, f32[16,8,1024]{2,1,0:T(8,128)}, f32[16,1024]{1,0:T(8,128)S(1)}, /*i...) while((s32[]{:T(128)}, f32[16,1024]{1,0:T(8,128)S(1)}, ...), condition=%wide.region_14.15_spmd, body=%wide.region_5.14_spmd.sunk | while | flops 1441801 | bytes 1316385 | solution.py:36
  119.4 1.3 constant_dynamic-slice_fusion.40
  124.4 1.4 constant_dynamic-slice_fusion.40
  136.9 1.5 constant_dynamic-slice_fusion.40
  139.6 1.3 constant_dynamic-slice_fusion.40
  144.6 1.3 constant_dynamic-slice_fusion.40
  159.6 2.5 fusion.58
  162.2 21.8 %all-gather.7.cloned.1.call-done = bf16[1024,4096]{1,0:T(8,128)(2,1)} async-done(((bf16[1024,128]{1,0:T(8,128)(2,1)}), bf16[1024,4096]{1,0:T(8,128)(2,1)}) %all-gather.7.cloned.1.call-update) | async-done | bytes 8388624 | tf_op jit(solution)/shard_map/all_gather | solution.py:86
  184.0 5.7 %convolution_convert_fusion.1 = bf16[128,4096]{1,0:T(8,128)(2,1)} fusion(bf16[128,1024]{1,0:T(8,128)(2,1)S(1)} %fusion.58, bf16[1024,4096]{1,0:T(8,128)(2,1)} %all-gather.7.cloned.1.call-done), kind=kOutput, calls=%fused_computation.111 | convolution fusion | flops 1074266112 | bytes 9699328 | tf_op jit(solution)/shard_map/dot_general | solution.py:88
  191.4 41.3 %reduce-scatter.3.cloned.1.call-done = bf16[16,4096]{1,0:T(8,128)(2,1)} async-done(((bf16[128,4096]{1,0:T(8,128)(2,1)}), bf16[16,4096]{1,0:T(8,128)(2,1)}) %reduce-scatter.3.cloned.1.call-update) | async-done | bytes 131088 | tf_op jit(solution)/shard_map/reduce_scatter | solution.py:87
  238.6 18.0 %all_to_all.10 = bf16[8,5,4096]{2,1,0:T(8,128)(2,1)} all-to-all(bf16[8,5,4096]{2,1,0:T(8,128)(2,1)} %reshape.357), channel_id=1, replica_groups=mesh['seq'=32,'exp'=8] {'exp'}, dimensions={0} | all-to-all | bytes 655360 | tf_op jit(solution)/shard_map/all_to_all | solution.py:117
  256.5 1.9 reshape.358
  258.5 59.5 %all-gather.9.cloned.1.call-done = bf16[1280,4096]{1,0:T(8,128)(2,1)} async-done(((bf16[40,4096]{1,0:T(8,128)(2,1)}), bf16[1280,4096]{1,0:T(8,128)(2,1)}) %all-gather.9.cloned.1.call-update) | async-done | bytes 10485776 | tf_op jit(solution)/shard_map/all_gather | solution.py:119
  318.0 10.2 %fusion.33 = f32[1280,384]{1,0:T(8,128)} fusion(bf16[1280,4096]{1,0:T(8,128)(2,1)} %all-gather.9.cloned.1.call-done, bf16[1,4096,384]{2,1,0:T(8,128)(2,1)} %param.37), kind=kOutput, calls=%fused_computation.116 | convolution fusion | flops 4026531840 | bytes 15597568 | tf_op jit(solution)/shard_map/dot_general | solution.py:120
  328.2 17.2 %convolution_convert_fusion = bf16[1280,4096]{1,0:T(8,128)(2,1)} fusion(bf16[1,384,4096]{2,1,0:T(8,128)(2,1)S(1)} %copy-done, bf16[1280,4096]{1,0:T(8,128)(2,1)} %all-gather.9.cloned.1.call-done, bf16[1,4096,384]{2,1,0:T(8,128)(2,1)} %param.38, f32[1280,384]{1,0:T(8,128)} %fusion.33), kind=kOutput, calls=%fused_computation.110 | convolution fusion | flops 8061255680 | bytes 29229056 | tf_op jit(solution)/shard_map/dot_general | solution.py:123
  345.4 105.2 %reduce-scatter.5.cloned.1.call-done = bf16[40,4096]{1,0:T(8,128)(2,1)} async-done(((bf16[1280,4096]{1,0:T(8,128)(2,1)}), bf16[40,4096]{1,0:T(8,128)(2,1)}) %reduce-scatter.5.cloned.1.call-update) | async-done | bytes 327696 | tf_op jit(solution)/shard_map/reduce_scatter | solution.py:124
  450.6 1.9 reshape.359
  452.5 7.0 %all-to-all-start.1 = ((bf16[8,5,4096]{2,1,0:T(8,128)(2,1)}), bf16[8,5,4096]{2,1,0:T(8,128)(2,1)}, u32[]{:S(2)}, u32[]{:S(2)}) async-start(bf16[8,5,4096]{2,1,0:T(8,128)(2,1)} %reshape.359), calls=%async_computation.3 | async-start | bytes 1048576 | tf_op jit(solution)/shard_map/all_to_all | solution.py:127
  459.9 16.1 %all-to-all-done.1 = bf16[8,5,4096]{2,1,0:T(8,128)(2,1)} async-done(((bf16[8,5,4096]{2,1,0:T(8,128)(2,1)}), bf16[8,5,4096]{2,1,0:T(8,128)(2,1)}, u32[]{:S(2)}, u32[]{:S(2)}) %all-to-all-start.1) | async-done | bytes 327712 | tf_op jit(solution)/shard_map/all_to_all | solution.py:127
  477.4 1.7 fusion.64
  (287 shorter events, 68.6 us)
Async XLA Ops:
  7.2 321.0 %copy-start = (bf16[1,384,4096]{2,1,0:T(8,128)(2,1)S(1)}, bf16[1,384,4096]{2,1,0:T(8,128)(2,1)}, u32[]{:S(2)}) copy-start(bf16[1,384,4096]{2,1,0:T(8,128)(2,1)} %param.39) | copy-start | bytes 9437188
  7.2 12.0 %copy-start.2 = (f32[16,1024]{1,0:T(8,128)S(1)}, f32[16,1024]{1,0:T(8,128)}, u32[]{:S(2)}) copy-start(f32[16,1024]{1,0:T(8,128)} %param.28) | copy-start | bytes 196612
  7.2 59.0 %all-gather.11.cloned.1.call-start = ((), (), s32[]{:S(2)}) async-start(), calls=%async_computation.8 | async-start | bytes 2162688 | tf_op jit(solution)/shard_map/all_gather | solution.py:17
  8.1 7.4 %collective-permute-start = (bf16[3,1024]{1,0:T(4,128)(2,1)S(1)}, bf16[3,1024]{1,0:T(4,128)(2,1)S(1)}, u32[]{:S(2)}, u32[]{:S(2)}) collective-permute-start(bf16[3,1024]{1,0:T(4,128)(2,1)S(1)} %slice.264), channel_id=1, source_target_pairs={{0,8},{8,16},{16,24},{24,32},{32,40},{40,48},{48,56},{56,64},{64,7... | collective-permute-start | bytes 18440 | tf_op jit(solution)/shard_map/ppermute | solution.py:12
  13.8 103.8 %all-gather.13.cloned.1.call-start = ((), (), s32[]{:S(2)}) async-start(), calls=%async_computation.9 | async-start | bytes 2162688 | tf_op jit(solution)/shard_map/all_gather | solution.py:17
  16.5 0.8 copy-start.1
  16.5 29.0 %copy-start.12 = (bf16[128,16]{0,1:T(8,128)(2,1)S(1)}, bf16[128,16]{0,1:T(8,128)(2,1)}, u32[]{:S(2)}) copy-start(bf16[128,16]{0,1:T(8,128)(2,1)} %param.27) | copy-start | bytes 12292
  44.0 0.6 copy-start.3
  44.7 139.3 %all-gather.7.cloned.1.call-start = ((), (), s32[]{:S(2)}) async-start(), calls=%async_computation.4 | async-start | bytes 8650752 | tf_op jit(solution)/shard_map/all_gather | solution.py:86
  45.4 187.3 %reduce-scatter.3.cloned.1.call-start = ((), (), s32[]{:S(2)}) async-start(), calls=%async_computation.5 | async-start | bytes 1179648 | tf_op jit(solution)/shard_map/reduce_scatter | solution.py:87
  119.3 40.3 %copy-start.9 = (f32[1024]{0:T(1024)S(1)}, f32[1024]{0:T(1024)}, u32[]{:S(2)}) copy-start(f32[1024]{0:T(1024)} %param.30) | copy-start | bytes 12292
  119.4 40.3 %copy-start.11 = (f32[1024]{0:T(1024)S(1)}, f32[1024]{0:T(1024)}, u32[]{:S(2)}) copy-start(f32[1024]{0:T(1024)} %param.31) | copy-start | bytes 12292
  162.2 27.5 %copy-start.4 = (bf16[128,1024]{1,0:T(8,128)(2,1)}, bf16[128,1024]{1,0:T(8,128)(2,1)S(1)}, u32[]{:S(2)}) copy-start(bf16[128,1024]{1,0:T(8,128)(2,1)S(1)} %fusion.58) | copy-start | bytes 786436
  162.2 70.5 %copy-start.7 = (bf16[16,4096]{1,0:T(8,128)(2,1)S(1)}, bf16[16,4096]{1,0:T(8,128)(2,1)}, u32[]{:S(2)}) copy-start(bf16[16,4096]{1,0:T(8,128)(2,1)} %param.33) | copy-start | bytes 393220
  162.2 71.6 %copy-start.10 = (f32[4096]{0:T(1024)S(1)}, f32[4096]{0:T(1024)}, u32[]{:S(2)}) copy-start(f32[4096]{0:T(1024)} %param.34) | copy-start | bytes 49156
  189.7 128.3 %all-gather.9.cloned.1.call-start = ((), (), s32[]{:S(2)}) async-start(), calls=%async_computation.6 | async-start | bytes 10813440 | tf_op jit(solution)/shard_map/all_gather | solution.py:119
  234.8 0.7 copy-start.5
  258.5 192.2 %reduce-scatter.5.cloned.1.call-start = ((), (), s32[]{:S(2)}) async-start(), calls=%async_computation.7 | async-start | bytes 10813440 | tf_op jit(solution)/shard_map/reduce_scatter | solution.py:124
  345.4 114.2 %copy-start.14 = (s32[32]{0:T(128)S(1)}, s32[32]{0:T(128)}, u32[]{:S(2)}) copy-start(s32[32]{0:T(128)} %multiply_add_fusion.8) | copy-start | bytes 388
  345.4 114.3 %copy-start.6 = (bf16[16,4096]{1,0:T(8,128)(2,1)S(1)}, bf16[16,4096]{1,0:T(8,128)(2,1)}, u32[]{:S(2)}) copy-start(bf16[16,4096]{1,0:T(8,128)(2,1)} %copy-done.5) | copy-start | bytes 393220
  345.4 114.3 %copy-start.8 = (bf16[4096,8]{0,1:T(8,128)(2,1)S(1)}, bf16[4096,8]{0,1:T(8,128)(2,1)}, u32[]{:S(2)}) copy-start(bf16[4096,8]{0,1:T(8,128)(2,1)} %param.35) | copy-start | bytes 196612
  345.4 114.4 %copy-start.13 = (s32[16,2]{0,1:T(2,128)S(1)}, s32[16,2]{0,1:T(2,128)}, u32[]{:S(2)}) copy-start(s32[16,2]{0,1:T(2,128)} %param.36) | copy-start | bytes 388
  452.5 23.4 %all-to-all-start.1 = ((bf16[8,5,4096]{2,1,0:T(8,128)(2,1)}), bf16[8,5,4096]{2,1,0:T(8,128)(2,1)}, u32[]{:S(2)}, u32[]{:S(2)}) async-start(bf16[8,5,4096]{2,1,0:T(8,128)(2,1)} %reshape.359), calls=%async_computation.3 | async-start | bytes 1048576 | tf_op jit(solution)/shard_map/all_to_all | solution.py:127
Sparse Core Ops, SparseCore 0:
  13.9 52.2 all-gather.10
  69.3 48.1 all-gather.12
  120.0 63.9 all-gather.6
  189.8 42.8 reduce-scatter.2
  258.6 59.3 all-gather.8
  345.5 105.0 reduce-scatter.4
where the time goes:
time: 492 us; the launch traced here: 486 us
  waiting for transfers between devices  317 us (64%)
  other arithmetic  67.9 us (14%)
  matrix products  34.6 us (7%)
  local copies, waits for them, and re-layouts  24 us (5%)
  blocking collectives  18 us (4%)
  between operations  14.4 us (3%)
  starting transfers between devices  9.3 us (2%)
    reduce_scatter x1, waiting for transfers between devices, shards(): lax.psum_scatter(partial_out.astype(jnp.bfloat16), 'seq', scatter_dimensi...  105 us
    all_gather x2, waiting for transfers between devices, carried_in(): gathered = jax.tree.map(lambda a: lax.all_gather(a, axis), part)  71.9 us
    all_gather x1, waiting for transfers between devices, shards(): piece = lax.all_gather(flat_rows, 'seq', axis=0, tiled=True)  59.5 us
    slice x32, other arithmetic, sweep(): lax.scan(advance, state, (delta, convolved, input_rows, output_rows), unr...  42.6 us
    reduce_scatter x1, waiting for transfers between devices, shards(): lax.psum_scatter(jnp.dot(mixed, full_weight, preferred_element_type=jnp.f...  41.3 us
    all_gather x1, waiting for transfers between devices, shards(): full_weight = lax.all_gather(out_weight, 'seq', axis=1, tiled=True)  21.8 us
    all_to_all x1, blocking collectives, shards(): lax.all_to_all(outgoing, 'exp', split_axis=0, concat_axis=0, tiled=True)  18 us
    dot_general x1, matrix products, shards(): jnp.dot(activated, down_weight[0], preferred_element_type=jnp.float32)  17.2 us
  transfers between devices with their start and end apart: 8, of which 7 were waited for; matrix products, arithmetic and copies ran while one was open for 16% of the time, Pallas kernels for 0%

commit v1 on v0

--- a/solution.py
+++ b/solution.py
@@ -1,9 +1,20 @@
+import functools
 import jax
 import jax.numpy as jnp
 from jax import lax
 from jax.sharding import PartitionSpec as P
 
 KCONV = 4
+
+
+def drive_the_keys(raw, mesh_ax):
+    w2 = lax.axis_size(mesh_ax)
+    top = jnp.stack([raw] * w2)
+    item_now = lax.all_to_all(top, mesh_ax, 0, 0)
+    return jnp.concatenate(item_now, axis=1)
+
+
+bind_strings = functools.partial(drive_the_keys, mesh_ax="seq")
 
 
 def from_behind(block, axis, distance):
@@ -83,7 +94,7 @@
     ).astype(jnp.bfloat16)
     rows = residual.shape[0]
     model_width = residual.shape[1]
-    full_weight = lax.all_gather(out_weight, "seq", axis=1, tiled=True)
+    full_weight = bind_strings(out_weight)
     projected = lax.psum_scatter(
         jnp.dot(mixed, full_weight, preferred_element_type=jnp.float32).astype(jnp.bfloat16),
         "exp",

time: 492 us -> 545 us (1.11)
  waiting for transfers between devices: 317 us -> 355 us
  starting transfers between devices: 9.3 us -> 18.1 us
    all_gather x2, waiting for transfers between devices: 71.9 us -> 110 us  [carried_in(): gathered = jax.tree.map(lambda a: lax.all_gather(a, axis), part)]
    reduce_scatter x1, waiting for transfers between devices: 41.3 us -> 64.1 us  [shards(): lax.psum_scatter(jnp.dot(mixed, full_weight, preferred_element_type=jnp.f...]
    all_gather x1 -> x0, waiting for transfers between devices: 21.8 us -> none  [shards(): full_weight = lax.all_gather(out_weight, 'seq', axis=1, tiled=True)]
    all_to_all x0 -> x1, starting transfers between devices: none -> 8.71 us  [drive_the_keys(): item_now = lax.all_to_all(top, mesh_ax, 0, 0)]
  transfers between devices with their start and end apart: 8 -> 8, of which waited for: 7 -> 6; matrix products, arithmetic and copies ran while one was open for 16% -> 15% of each run, Pallas kernels for 0% -> 0%
where the time goes in v1:
time: 545 us; the launch traced here: 539 us
  waiting for transfers between devices  355 us (65%)
  other arithmetic  67.3 us (12%)
  matrix products  36.4 us (7%)
  local copies, waits for them, and re-layouts  29.3 us (5%)
  starting transfers between devices  18.1 us (3%)
  blocking collectives  18 us (3%)
  between operations  14 us (3%)
    all_gather x2, waiting for transfers between devices, carried_in(): gathered = jax.tree.map(lambda a: lax.all_gather(a, axis), part)  110 us
    reduce_scatter x1, waiting for transfers between devices, shards(): lax.psum_scatter(partial_out.astype(jnp.bfloat16), 'seq', scatter_dimensi...  105 us
    reduce_scatter x1, waiting for transfers between devices, shards(): lax.psum_scatter(jnp.dot(mixed, full_weight, preferred_element_type=jnp.f...  64.1 us
    all_gather x1, waiting for transfers between devices, shards(): piece = lax.all_gather(flat_rows, 'seq', axis=0, tiled=True)  59.3 us
    slice x32, other arithmetic, sweep(): lax.scan(advance, state, (delta, convolved, input_rows, output_rows), unr...  42.6 us
    all_to_all x1, blocking collectives, shards(): lax.all_to_all(outgoing, 'exp', split_axis=0, concat_axis=0, tiled=True)  18 us
    dot_general x1, matrix products, shards(): jnp.dot(activated, down_weight[0], preferred_element_type=jnp.float32)  17.2 us
    all_to_all x1, waiting for transfers between devices, shards(): lax.all_to_all(summed_out.reshape(arrived.shape), 'exp', split_axis=0, co...  16.1 us
  transfers between devices with their start and end apart: 8, of which 6 were waited for; matrix products, arithmetic and copies ran while one was open for 15% of the time, Pallas kernels for 0%

profile of v1, /device:TPU:2, one launch (start us, length us, event | category | flops | bytes accessed | tf_op | source)
XLA Modules:
  0.0 539.2 jit_solution(2513918077394352957)
XLA Ops:
  8.1 2.0 collective-permute-start
  10.2 2.1 fusion.59
  12.2 1.5 multiply_exponential_fusion
  17.3 1.8 fusion.81
  19.2 24.9 %while.37 = (s32[]{:T(128)}, f32[16,1024]{1,0:T(8,128)S(1)}, f32[16,8,1024]{2,1,0:T(8,128)}, f32[16,1024]{1,0:T(8,128)S(1)}, f32[16,8,16]{2,1,0:T(8,128)S(1)}, /...) while((s32[]{:T(128)}, f32[16,1024]{1,0:T(8,128)S(1)}, ...), condition=%wide.region_2.3_spmd.clone, body=%wide.region_1.2_spmd.clone.sunk | while | flops 811018 | bytes 396055 | solution.py:47
  26.8 1.4 constant_dynamic-slice_fusion.41
  33.0 1.5 constant_dynamic-slice_fusion.41
  34.8 1.3 constant_dynamic-slice_fusion.41
  41.0 1.4 constant_dynamic-slice_fusion.41
  45.8 4.3 stack.2
  50.1 8.7 %all-to-all-start = ((bf16[32,1024,128]{1,2,0:T(8,128)(2,1)}), bf16[32,1024,128]{1,2,0:T(8,128)(2,1)}, u32[]{:S(2)}, u32[]{:S(2)}) async-start(bf16[32,1024,128]{1,2,0:T(8,128)(2,1)} %stack.2), calls=%async_computation | async-start | bytes 16777216 | tf_op jit(solution)/shard_map/all_to_all | solution.py:13
  59.0 9.3 %all-gather.8.cloned.1.call-done = f32[512,1024]{1,0:T(8,128)} async-done(((f32[16,1024]{1,0:T(8,128)}), f32[512,1024]{1,0:T(8,128)}) %all-gather.8.cloned.1.call-update) | async-done | bytes 2097168 | tf_op jit(solution)/shard_map/all_gather | solution.py:28
  68.3 100.7 %all-gather.10.cloned.1.call-done = f32[512,1024]{1,0:T(8,128)} async-done(((f32[16,1024]{1,0:T(8,128)}), f32[512,1024]{1,0:T(8,128)}) %all-gather.10.cloned.1.call-update) | async-done | bytes 2097168 | tf_op jit(solution)/shard_map/all_gather | solution.py:28
  169.0 1.8 while.35
  170.8 40.3 %while.36 = (s32[]{:T(128)}, f32[16,1024]{1,0:T(8,128)S(1)}, f32[16,8,1024]{2,1,0:T(8,128)}, f32[16,8,1024]{2,1,0:T(8,128)}, f32[16,1024]{1,0:T(8,128)S(1)}, /*i...) while((s32[]{:T(128)}, f32[16,1024]{1,0:T(8,128)S(1)}, ...), condition=%wide.region_14.15_spmd, body=%wide.region_5.14_spmd.sunk | while | flops 1441801 | bytes 1316385 | solution.py:47
  183.4 1.4 constant_dynamic-slice_fusion.40
  193.4 1.5 constant_dynamic-slice_fusion.40
  196.1 1.3 constant_dynamic-slice_fusion.40
  206.1 1.4 constant_dynamic-slice_fusion.40
  211.1 2.4 fusion.58
  213.6 7.4 %convolution_convert_fusion.1 = bf16[128,4096]{1,0:T(8,128)(2,1)} fusion(bf16[128,1024]{1,0:T(8,128)(2,1)S(1)} %fusion.58, bf16[1024,4096]{0,1:T(8,128)(2,1)} %bitcast.55), kind=kOutput, calls=%fused_computation.111 | convolution fusion | flops 1074266112 | bytes 9699328 | tf_op jit(solution)/shard_map/dot_general | solution.py:99
  222.2 64.1 %reduce-scatter.3.cloned.1.call-done = bf16[16,4096]{1,0:T(8,128)(2,1)} async-done(((bf16[128,4096]{1,0:T(8,128)(2,1)}), bf16[16,4096]{1,0:T(8,128)(2,1)}) %reduce-scatter.3.cloned.1.call-update) | async-done | bytes 131088 | tf_op jit(solution)/shard_map/reduce_scatter | solution.py:98
  292.1 18.0 %all_to_all.15 = bf16[8,5,4096]{2,1,0:T(8,128)(2,1)} all-to-all(bf16[8,5,4096]{2,1,0:T(8,128)(2,1)} %reshape.367), channel_id=1, replica_groups=mesh['seq'=32,'exp'=8] {'exp'}, dimensions={0} | all-to-all | bytes 655360 | tf_op jit(solution)/shard_map/all_to_all | solution.py:128
  310.1 1.9 reshape.368
  312.3 59.3 %all-gather.6.cloned.1.call-done = bf16[1280,4096]{1,0:T(8,128)(2,1)} async-done(((bf16[40,4096]{1,0:T(8,128)(2,1)}), bf16[1280,4096]{1,0:T(8,128)(2,1)}) %all-gather.6.cloned.1.call-update) | async-done | bytes 10485776 | tf_op jit(solution)/shard_map/all_gather | solution.py:130
  371.6 10.2 %fusion.33 = f32[1280,384]{1,0:T(8,128)} fusion(bf16[1280,4096]{1,0:T(8,128)(2,1)} %all-gather.6.cloned.1.call-done, bf16[1,4096,384]{2,1,0:T(8,128)(2,1)} %param.37), kind=kOutput, calls=%fused_computation.116 | convolution fusion | flops 4026531840 | bytes 15597568 | tf_op jit(solution)/shard_map/dot_general | solution.py:131
  381.8 17.2 %convolution_convert_fusion = bf16[1280,4096]{1,0:T(8,128)(2,1)} fusion(bf16[1,384,4096]{2,1,0:T(8,128)(2,1)S(1)} %copy-done, bf16[1280,4096]{1,0:T(8,128)(2,1)} %all-gather.6.cloned.1.call-done, bf16[1,4096,384]{2,1,0:T(8,128)(2,1)} %param.38, f32[1280,384]{1,0:T(8,128)} %fusion.33), kind=kOutput, calls=%fused_computation.110 | convolution fusion | flops 8061255680 | bytes 29229056 | tf_op jit(solution)/shard_map/dot_general | solution.py:134
  399.0 105.2 %reduce-scatter.5.cloned.1.call-done = bf16[40,4096]{1,0:T(8,128)(2,1)} async-done(((bf16[1280,4096]{1,0:T(8,128)(2,1)}), bf16[40,4096]{1,0:T(8,128)(2,1)}) %reduce-scatter.5.cloned.1.call-update) | async-done | bytes 327696 | tf_op jit(solution)/shard_map/reduce_scatter | solution.py:135
  504.2 1.9 reshape.369
  506.1 7.0 %all-to-all-start.2 = ((bf16[8,5,4096]{2,1,0:T(8,128)(2,1)}), bf16[8,5,4096]{2,1,0:T(8,128)(2,1)}, u32[]{:S(2)}, u32[]{:S(2)}) async-start(bf16[8,5,4096]{2,1,0:T(8,128)(2,1)} %reshape.369), calls=%async_computation.4 | async-start | bytes 1048576 | tf_op jit(solution)/shard_map/all_to_all | solution.py:138
  513.5 16.1 %all-to-all-done.2 = bf16[8,5,4096]{2,1,0:T(8,128)(2,1)} async-done(((bf16[8,5,4096]{2,1,0:T(8,128)(2,1)}), bf16[8,5,4096]{2,1,0:T(8,128)(2,1)}, u32[]{:S(2)}, u32[]{:S(2)}) %all-to-all-start.2) | async-done | bytes 327712 | tf_op jit(solution)/shard_map/all_to_all | solution.py:138
  531.0 1.7 fusion.64
  (282 shorter events, 69.8 us)
Async XLA Ops:
  7.2 374.6 %copy-start = (bf16[1,384,4096]{2,1,0:T(8,128)(2,1)S(1)}, bf16[1,384,4096]{2,1,0:T(8,128)(2,1)}, u32[]{:S(2)}) copy-start(bf16[1,384,4096]{2,1,0:T(8,128)(2,1)} %param.39) | copy-start | bytes 9437188
  7.2 12.0 %copy-start.2 = (f32[16,1024]{1,0:T(8,128)S(1)}, f32[16,1024]{1,0:T(8,128)}, u32[]{:S(2)}) copy-start(f32[16,1024]{1,0:T(8,128)} %param.28) | copy-start | bytes 196612
  7.2 61.1 %all-gather.8.cloned.1.call-start = ((), (), s32[]{:S(2)}) async-start(), calls=%async_computation.8 | async-start | bytes 2162688 | tf_op jit(solution)/shard_map/all_gather | solution.py:28
  8.1 7.4 %collective-permute-start = (bf16[3,1024]{1,0:T(4,128)(2,1)S(1)}, bf16[3,1024]{1,0:T(4,128)(2,1)S(1)}, u32[]{:S(2)}, u32[]{:S(2)}) collective-permute-start(bf16[3,1024]{1,0:T(4,128)(2,1)S(1)} %slice.264), channel_id=1, source_target_pairs={{0,8},{8,16},{16,24},{24,32},{32,40},{40,48},{48,56},{56,64},{64,7... | collective-permute-start | bytes 18440 | tf_op jit(solution)/shard_map/ppermute | solution.py:23
  13.7 155.3 %all-gather.10.cloned.1.call-start = ((), (), s32[]{:S(2)}) async-start(), calls=%async_computation.9 | async-start | bytes 2162688 | tf_op jit(solution)/shard_map/all_gather | solution.py:28
  16.5 0.8 copy-start.1
  44.0 0.6 copy-start.3
  50.1 8.8 %copy-start.10 = (bf16[128,16]{0,1:T(8,128)(2,1)S(1)}, bf16[128,16]{0,1:T(8,128)(2,1)}, u32[]{:S(2)}) copy-start(bf16[128,16]{0,1:T(8,128)(2,1)} %param.27) | copy-start | bytes 12292
  50.1 163.5 %all-to-all-start = ((bf16[32,1024,128]{1,2,0:T(8,128)(2,1)}), bf16[32,1024,128]{1,2,0:T(8,128)(2,1)}, u32[]{:S(2)}, u32[]{:S(2)}) async-start(bf16[32,1024,128]{1,2,0:T(8,128)(2,1)} %stack.2), calls=%async_computation | async-start | bytes 16777216 | tf_op jit(solution)/shard_map/all_to_all | solution.py:13
  58.8 227.5 %reduce-scatter.3.cloned.1.call-start = ((), (), s32[]{:S(2)}) async-start(), calls=%async_computation.5 | async-start | bytes 1179648 | tf_op jit(solution)/shard_map/reduce_scatter | solution.py:98
  213.5 7.5 %copy-start.7 = (bf16[128,1024]{1,0:T(8,128)(2,1)}, bf16[128,1024]{1,0:T(8,128)(2,1)S(1)}, u32[]{:S(2)}) copy-start(bf16[128,1024]{1,0:T(8,128)(2,1)S(1)} %fusion.58) | copy-start | bytes 786436
  213.6 72.7 %copy-start.6 = (bf16[16,4096]{1,0:T(8,128)(2,1)S(1)}, bf16[16,4096]{1,0:T(8,128)(2,1)}, u32[]{:S(2)}) copy-start(bf16[16,4096]{1,0:T(8,128)(2,1)} %param.33) | copy-start | bytes 393220
  213.6 73.8 %copy-start.9 = (f32[4096]{0:T(1024)S(1)}, f32[4096]{0:T(1024)}, u32[]{:S(2)}) copy-start(f32[4096]{0:T(1024)} %param.34) | copy-start | bytes 49156
  221.1 150.5 %all-gather.6.cloned.1.call-start = ((), (), s32[]{:S(2)}) async-start(), calls=%async_computation.6 | async-start | bytes 10813440 | tf_op jit(solution)/shard_map/all_gather | solution.py:130
  288.4 0.7 copy-start.4
  312.1 192.2 %reduce-scatter.5.cloned.1.call-start = ((), (), s32[]{:S(2)}) async-start(), calls=%async_computation.7 | async-start | bytes 10813440 | tf_op jit(solution)/shard_map/reduce_scatter | solution.py:135
  399.0 114.3 %copy-start.5 = (bf16[16,4096]{1,0:T(8,128)(2,1)S(1)}, bf16[16,4096]{1,0:T(8,128)(2,1)}, u32[]{:S(2)}) copy-start(bf16[16,4096]{1,0:T(8,128)(2,1)} %copy-done.4) | copy-start | bytes 393220
  399.0 114.3 %copy-start.8 = (bf16[4096,8]{0,1:T(8,128)(2,1)S(1)}, bf16[4096,8]{0,1:T(8,128)(2,1)}, u32[]{:S(2)}) copy-start(bf16[4096,8]{0,1:T(8,128)(2,1)} %param.35) | copy-start | bytes 196612
  399.0 114.4 %copy-start.11 = (s32[16,2]{0,1:T(2,128)S(1)}, s32[16,2]{0,1:T(2,128)}, u32[]{:S(2)}) copy-start(s32[16,2]{0,1:T(2,128)} %param.36) | copy-start | bytes 388
  506.1 23.4 %all-to-all-start.2 = ((bf16[8,5,4096]{2,1,0:T(8,128)(2,1)}), bf16[8,5,4096]{2,1,0:T(8,128)(2,1)}, u32[]{:S(2)}, u32[]{:S(2)}) async-start(bf16[8,5,4096]{2,1,0:T(8,128)(2,1)} %reshape.369), calls=%async_computation.4 | async-start | bytes 1048576 | tf_op jit(solution)/shard_map/all_to_all | solution.py:138
Sparse Core Ops, SparseCore 0:
  13.9 54.4 all-gather.7
  71.4 97.5 all-gather.9
  221.2 65.0 reduce-scatter.2
  312.2 59.3 all-gather.5
  399.1 105.0 reduce-scatter.4
